TPU v7x, 128 devices: a whole 4x4x4 slice. The times are simulated.
128 devices in a mesh: tier: 8 (over y, z_lo), tile: 16 (over x, z_hi, core).
Axes of the slice: x: 4, y: 4, z: 4 (z_hi: 2, z_lo: 2; z = z_hi * 2 + z_lo), core: 2. Of those that a mesh axis runs over, the one named last changes fastest.
Arguments:
- warming_above_ambient: float32 [8, 16, 512, 2048], P('tier', None, 'tile'), may hold values from -6 to 6
- substance_label: int32 [8, 16, 512, 2048], P('tier', None, 'tile'), may hold values from 0 to 15
- glue_zone_label: int32 [512, 2048], P('tile'), may hold values from 0 to 7
- patch_label_per_cell: int32 [8, 512, 2048], P('tier', 'tile'), may hold values from 0 to 127
- heat_conductance_per_substance: float32 [16], replicated, may hold values from 0.3 to 4
- dissipation_per_patch: float32 [8, 128], P('tier'), may hold values from 0.5 to 5
- glue_sheet_reciprocal_operators: float32 [8, 16, 16], replicated, may hold values from -0.3 to 1.3, as said below
Outputs:
- final_state: float32 [8, 16, 512, 2048], P('tier', None, 'tile')
Inputs may be any that keep to these rules, and one draw needn't show every extreme that they name: `glue_sheet_reciprocal_operators`: each matrix has diagonal entries of 0.6 to 1.0 plus a perturbation, and perturbed entries elsewhere.
All inputs are finite; a program needn't handle non-finite values.
Results may differ from a plain program's by a relative error of at most 0.0001.
Values sent between devices are 32-bit elements; how exact they have to be, the bound alone decides.
A program may use at most 128 MiB of HBM per device.

v0:
```python
import jax
import jax.numpy as jnp
from jax import lax
from jax.sharding import PartitionSpec as P

MATERIALS = 16
REGIONS = 8
POWER_TILES = 128
STEPS = 2
step_dt = 0.04


def padded(cells, sides, width):
    for axis, dim in sides:
        count = lax.axis_size(axis)
        ends = count - 1
        head = lax.slice_in_dim(cells, 0, width, axis=dim)
        tail = lax.slice_in_dim(cells, cells.shape[dim] - width, cells.shape[dim], axis=dim)
        cells = jnp.concatenate(
            [
                lax.ppermute(tail, axis, [(i, (i + 1) % count) for i in range(ends)]),
                cells,
                lax.ppermute(head, axis, [((i + 1) % count, i) for i in range(ends)]),
            ],
            axis=dim,
        )
    return cells


def pad_axis(field, axis, low, high):
    widths = [(0, 0)] * field.ndim
    widths[axis] = (low, high)
    return jnp.pad(field, widths)


def conduct(padded_t, padded_k):
    centre = padded_t[..., 1:-1, :]
    kcell = padded_k[..., 1:-1, :]
    flux = 0.5 * (kcell + padded_k[..., 2:, :]) * (padded_t[..., 2:, :] - centre)
    flux = flux + 0.5 * (kcell + padded_k[..., :-2, :]) * (padded_t[..., :-2, :] - centre)
    side_t = pad_axis(centre, centre.ndim - 1, 1, 1)
    side_k = pad_axis(kcell, kcell.ndim - 1, 1, 1)
    flux = flux + 0.5 * (kcell + side_k[..., 2:]) * (side_t[..., 2:] - centre)
    flux = flux + 0.5 * (kcell + side_k[..., :-2]) * (side_t[..., :-2] - centre)
    face = (
        0.5
        * (kcell[..., 1:, :, :] + kcell[..., :-1, :, :])
        * (centre[..., 1:, :, :] - centre[..., :-1, :, :])
    )
    axis = centre.ndim - 3
    return flux + pad_axis(face, axis, 0, 1) - pad_axis(face, axis, 1, 0)


def select_solve(matrices, planes, regions):
    solved = jnp.zeros((matrices.shape[1],) + planes.shape[1:], jnp.float32)
    for which in range(REGIONS):
        mapped = jnp.einsum("ij,jxc->ixc", matrices[which], planes, precision=lax.Precision.HIGHEST)
        solved = solved + jnp.where(regions == which, mapped, 0.0)
    return solved


def local(
    warming_above_ambient,
    substance_label,
    glue_zone_label,
    patch_label_per_cell,
    heat_conductance_per_substance,
    dissipation_per_patch,
    glue_sheet_reciprocal_operators,
):
    kappa = jnp.zeros(substance_label.shape, jnp.float32)
    for which in range(MATERIALS):
        kappa = jnp.where(substance_label == which, heat_conductance_per_substance[which], kappa)
    onehot = (patch_label_per_cell[0][..., None] == lax.iota(jnp.int32, POWER_TILES)).astype(
        jnp.float32
    )
    source = jnp.dot(
        onehot.reshape(-1, POWER_TILES), dissipation_per_patch[0], precision=lax.Precision.HIGHEST
    )
    source = source.reshape(patch_label_per_cell.shape[1:])
    tier_index = lax.axis_index("tier")
    heating_snapshot = warming_above_ambient
    for step in range(STEPS):
        joined = padded(jnp.stack([heating_snapshot, kappa]), (("tile", 3),), 1)
        padded_t = joined[0]
        padded_k = joined[1]
        heating_snapshot = heating_snapshot + step_dt * conduct(padded_t, padded_k)
        heating_snapshot = heating_snapshot.at[:, 0].add(step_dt * source)
        planes = jnp.stack([heating_snapshot[0, 0], heating_snapshot[0, -1]])
        gathered = lax.all_gather(planes, "tier", axis=0, tiled=True)
        own_rows = lax.dynamic_slice_in_dim(glue_sheet_reciprocal_operators, 2 * tier_index, 2, 1)
        updated = select_solve(own_rows, gathered, glue_zone_label)
        heating_snapshot = heating_snapshot.at[0, 0].set(updated[0]).at[0, -1].set(updated[1])
    return heating_snapshot


def solution(mesh):
    in_specs = (
        P("tier", None, "tile", None),
        P("tier", None, "tile", None),
        P("tile", None),
        P("tier", "tile", None),
        P(),
        P("tier", None),
        P(),
    )
    out_specs = P("tier", None, "tile", None)
    return jax.shard_map(local, mesh=mesh, in_specs=in_specs, out_specs=out_specs, check_vma=False)
```

profile of v0, /device:TPU:27, one launch (start us, length us, event | category | flops | bytes accessed | tf_op | source)
XLA Modules:
  0.0 563.4 jit_solution(4008973471089859055)
XLA Ops:
  6.5 1.9 fusion.178
  8.5 5.0 stack.22
  13.5 44.8 %fusion.8 = f32[1,1,16,32,2048]{4,0,3,2,1:T(1,128)S(1)} fusion(s32[1,16,32,2048]{3,2,1,0:T(8,128)S(1)} %copy-done.16, f32[]{:T(128)} %bitcast.15, f32[]{:T(128)} %bitcast.14, f32[]{:T(128)} %bitcast.13, f32[]{:T(128)} %bitcast.12, f32[]{:T(128)} %bitcast.11, f32[]{:T(128)} %bitcast.10, f32[]{:T(128)} %bitcast.9, f32[]{:T(128)} %bitcast.8, f32[]{:T(128)} %bitcast.7, ...), kind=kLoop, calls=%fused_computation.33 | loop fusion | flops 33554432 | bytes 8388672 | tf_op jit(solution)/shard_map/stack | solution.py:84
  58.9 6.1 %collective-permute-start = (f32[2,1,16,1,2048]{4,0,3,2,1:T(2,128)S(1)}, f32[2,1,16,1,2048]{4,0,3,2,1:T(2,128)S(1)}, u32[]{:S(2)}, u32[]{:S(2)}) collective-permute-start(f32[2,1,16,1,2048]{4,0,3,2,1:T(2,128)S(1)} %get-tuple-element.77), channel_id=1, source_target_pairs={{0,1},{1,2},{2,3},{3,4},{4,5},{5,6},{6,7},{7,8},{8,9},{9,10},{10,1... | collective-permute-start | bytes 786440 | tf_op jit(solution)/shard_map/ppermute | solution.py:21
  65.0 2.1 collective-permute-start.1
  67.1 23.6 %fusion.1 = f32[1,32,2048]{2,0,1:T(1,128)S(1)} fusion(s32[32,2048]{1,0:T(8,128)S(1)} %bitcast.110, f32[1,128]{1,0:T(1,128)S(1)} %copy-done.20), kind=kOutput, calls=%fused_computation.2 | convolution fusion | flops 109051904 | bytes 524800 | tf_op jit(solution)/shard_map/dot_general | solution.py:77
  90.8 8.0 %fusion.5 = f32[2,1,16,34,2048]{4,0,3,2,1:T(2,128)S(1)} fusion(f32[1,1,16,32,2048]{4,0,3,2,1:T(1,128)S(1)} %fusion.8, f32[2,1,16,1,2048]{4,0,3,2,1:T(2,128)S(1)} %collective-permute-done.1, f32[1,1,16,32,2048]{4,0,3,2,1:T(1,128)S(1)} %stack.22, f32[2,1,16,1,2048]{4,0,3,2,1:T(2,128)S(1)} %collective-permute-done), kind=kLoop, calls=%fused_computation.23 | loop fusion | flops 6684672 | bytes 17825792 | tf_op jit(solution)/shard_map/concatenate | solution.py:19
  98.8 7.9 %slice_bitcast_fusion.3 = (f32[1,16,34,2048]{3,0,2,1:T(1,128)S(1)}, f32[1,16,34,2048]{3,0,2,1:T(1,128)}) fusion(f32[2,1,16,34,2048]{4,0,3,2,1:T(2,128)S(1)} %fusion.5), kind=kLoop, calls=%fused_computation.32 | loop fusion | bytes 17825792 | tf_op jit(solution)/shard_map/squeeze | solution.py:86
  106.7 5.2 slice.452
  111.9 7.9 %slice.456 = f32[1,16,32,2048]{3,0,2,1:T(1,128)} slice(f32[1,16,34,2048]{3,0,2,1:T(1,128)} %get-tuple-element.84), slice={[0:1], [0:16], [1:33], [0:2048]} | slice | bytes 8388608 | tf_op jit(solution)/shard_map/slice | solution.py:37
  119.8 11.4 %fusion.21 = f32[1,15,32,2048]{3,0,2,1:T(1,128)S(1)} fusion(f32[1,16,34,2048]{3,0,2,1:T(1,128)} %get-tuple-element.84, f32[1,16,34,2048]{3,0,2,1:T(1,128)S(1)} %get-tuple-element.83), kind=kLoop, calls=%fused_computation.59 | loop fusion | flops 3932160 | bytes 19660800 | tf_op jit(solution)/shard_map/mul | solution.py:46
  131.2 46.0 %copy_add_fusion = f32[1,16,32,2048]{3,0,2,1:T(1,128)S(1)} fusion(f32[1,16,32,2048]{3,2,1,0:T(8,128)S(1)} %copy-done.11, f32[1,15,32,2048]{3,0,2,1:T(1,128)S(1)} %fusion.21, f32[1,16,32,2048]{3,0,2,1:T(1,128)S(1)} %copy-done.15, f32[1,16,32,2048]{3,0,2,1:T(1,128)S(1)} %copy-done.13, f32[1,16,34,2048]{3,0,2,1:T(1,128)} %get-tuple-element.84, ...), kind=kLoop, calls=%fused_computation.52 | loop fusion | flops 24117248 | bytes 37486592 | tf_op jit(solution)/shard_map/add | solution.py:87
  177.6 2.0 copy-done.3
  180.1 1.1 copy.61
  182.4 0.7 and_reduce_fusion
  183.5 90.0 %all-gather.3.cloned.1.call-done = f32[16,32,2048]{2,1,0:T(8,128)} async-done(((f32[2,32,2048]{2,1,0:T(8,128)}), f32[16,32,2048]{2,1,0:T(8,128)}) %all-gather.3.cloned.1.call-update) | async-done | bytes 4194320 | tf_op jit(solution)/shard_map/all_gather | solution.py:90
  273.5 6.8 %fusion.55 = f32[2,32,2048]{2,0,1:T(2,128)S(1)} fusion(f32[16,32,2048]{2,1,0:T(8,128)} %all-gather.3.cloned.1.call-done, pred[32,2048]{1,0:T(8,128)(4,1)S(1)} %get-tuple-element.99, f32[8,16,16]{2,1,0:T(8,128)S(1)} %copy-done, s32[]{:T(128)S(6)} %select_n.118), kind=kOutput, calls=%fused_computation.94 | convolution fusion | flops 25296896 | bytes 4785156 | tf_op jit(solution)/shard_map/ij,jxc->ixc/dot_general | solution.py:57
  280.2 4.7 fusion.142
  285.0 4.9 fusion.139
  289.9 4.7 fusion.136
  294.6 5.1 fusion.133
  299.8 4.7 fusion.130
  304.6 4.7 fusion.127
  309.3 4.9 fusion.124
  314.4 2.1 fusion.147
  316.9 3.9 collective-permute-start.2
  320.9 1.9 collective-permute-start.3
  322.8 1.4 collective-permute-done.2
  324.2 5.9 %collective-permute-done.3 = f32[2,1,16,1,2048]{4,0,3,2,1:T(2,128)S(1)} collective-permute-done((f32[2,1,16,1,2048]{4,0,3,2,1:T(2,128)S(1)}, f32[2,1,16,1,2048]{4,0,3,2,1:T(2,128)S(1)}, u32[]{:S(2)}, u32[]{:S(2)}) %collective-permute-start.3) | collective-permute-done | bytes 262176 | tf_op jit(solution)/shard_map/ppermute | solution.py:23
  330.1 8.1 %fusion.7 = f32[2,1,16,34,2048]{4,0,3,2,1:T(2,128)S(1)} fusion(f32[1,1,16,32,2048]{4,0,3,2,1:T(1,128)S(1)} %copy-done.8, f32[2,1,16,1,2048]{4,0,3,2,1:T(2,128)S(1)} %collective-permute-done.3, f32[1,1,16,32,2048]{4,0,3,2,1:T(1,128)S(1)} %bitcast.109, f32[2,1,16,1,2048]{4,0,3,2,1:T(2,128)S(1)} %collective-permute-done.2), kind=kLoop, calls=%fused_computation.25 | loop fusion | flops 6684672 | bytes 17825792 | tf_op jit(solution)/shard_map/concatenate | solution.py:19
  338.2 7.9 %slice_bitcast_fusion.1 = (f32[1,16,34,2048]{3,0,2,1:T(1,128)S(1)}, f32[1,16,34,2048]{3,0,2,1:T(1,128)}) fusion(f32[2,1,16,34,2048]{4,0,3,2,1:T(2,128)S(1)} %fusion.7), kind=kLoop, calls=%fused_computation.30 | loop fusion | bytes 17825792 | tf_op jit(solution)/shard_map/squeeze | solution.py:86
  346.1 5.2 slice.470
  351.3 7.9 %slice.474 = f32[1,16,32,2048]{3,0,2,1:T(1,128)} slice(f32[1,16,34,2048]{3,0,2,1:T(1,128)} %get-tuple-element.82), slice={[0:1], [0:16], [1:33], [0:2048]} | slice | bytes 8388608 | tf_op jit(solution)/shard_map/slice | solution.py:37
  359.2 11.4 %fusion.19 = f32[1,15,32,2048]{3,0,2,1:T(1,128)S(1)} fusion(f32[1,16,34,2048]{3,0,2,1:T(1,128)} %get-tuple-element.82, f32[1,16,34,2048]{3,0,2,1:T(1,128)S(1)} %get-tuple-element.81), kind=kLoop, calls=%fused_computation.55 | loop fusion | flops 3932160 | bytes 19660800 | tf_op jit(solution)/shard_map/mul | solution.py:46
  370.6 42.8 %multiply_add_fusion = f32[1,16,32,2048]{3,0,2,1:T(1,128)S(1)} fusion(f32[1,16,32,2048]{3,0,2,1:T(1,128)S(1)} %copy-done.6, f32[1,15,32,2048]{3,0,2,1:T(1,128)S(1)} %fusion.19, f32[1,16,32,2048]{3,0,2,1:T(1,128)S(1)} %copy-done.14, f32[1,16,32,2048]{3,0,2,1:T(1,128)S(1)} %copy-done.12, f32[1,16,34,2048]{3,0,2,1:T(1,128)} %get-tuple-element.82, ...), kind=kLoop, calls=%fused_computation.53 | loop fusion | flops 24117248 | bytes 37486592 | tf_op jit(solution)/shard_map/add | solution.py:87
  413.8 2.0 copy-done.9
  416.4 1.1 copy.70
  417.5 92.2 %all-gather.5.cloned.1.call-done = f32[16,32,2048]{2,1,0:T(8,128)} async-done(((f32[2,32,2048]{2,1,0:T(8,128)}), f32[16,32,2048]{2,1,0:T(8,128)}) %all-gather.5.cloned.1.call-update) | async-done | bytes 4194320 | tf_op jit(solution)/shard_map/all_gather | solution.py:90
  509.7 6.8 %fusion.79 = f32[2,32,2048]{2,0,1:T(2,128)S(1)} fusion(f32[16,32,2048]{2,1,0:T(8,128)} %all-gather.5.cloned.1.call-done, pred[32,2048]{1,0:T(8,128)(4,1)S(1)} %get-tuple-element.99, f32[8,16,16]{2,1,0:T(8,128)S(1)} %copy-done, s32[]{:T(128)S(6)} %select_n.118), kind=kOutput, calls=%fused_computation.102 | convolution fusion | flops 25296896 | bytes 4785156 | tf_op jit(solution)/shard_map/ij,jxc->ixc/dot_general | solution.py:57
  516.5 4.7 fusion.121
  521.2 4.9 fusion.118
  526.1 4.7 fusion.115
  530.9 5.0 fusion.112
  535.9 4.7 fusion.109
  540.6 4.7 fusion.106
  545.3 5.0 fusion.103
  550.6 1.7 fusion.148
  552.3 4.0 copy.79
  (60 shorter events, 4.8 us)
Async XLA Ops:
  6.5 266.9 %copy-start = (f32[8,16,16]{2,1,0:T(8,128)S(1)}, f32[8,16,16]{2,1,0:T(8,128)}, u32[]{:S(2)}) copy-start(f32[8,16,16]{2,1,0:T(8,128)} %param.25) | copy-start | bytes 24580
  6.5 266.9 %all-gather.3.cloned.1.call-start = ((), (), s32[]{:S(2)}) async-start(), calls=%async_computation | async-start | bytes 4718592 | tf_op jit(solution)/shard_map/all_gather | solution.py:90
  8.5 5.0 copy-start.16
  58.3 32.5 %copy-start.7 = (f32[1,1,16,32,2048]{4,0,3,2,1:T(1,128)}, f32[1,1,16,32,2048]{4,0,3,2,1:T(1,128)S(1)}, u32[]{:S(2)}) copy-start(f32[1,1,16,32,2048]{4,0,3,2,1:T(1,128)S(1)} %fusion.8) | copy-start | bytes 12582916
  58.3 8.8 %copy-start.19 = (s32[1,32,2048]{2,1,0:T(8,128)S(1)}, s32[1,32,2048]{2,1,0:T(8,128)}, u32[]{:S(2)}) copy-start(s32[1,32,2048]{2,1,0:T(8,128)} %param.22) | copy-start | bytes 786436
  58.3 8.8 %copy-start.20 = (f32[1,128]{1,0:T(1,128)S(1)}, f32[1,128]{1,0:T(1,128)}, u32[]{:S(2)}) copy-start(f32[1,128]{1,0:T(1,128)} %param.24) | copy-start | bytes 1540
  58.9 31.9 %collective-permute-start = (f32[2,1,16,1,2048]{4,0,3,2,1:T(2,128)S(1)}, f32[2,1,16,1,2048]{4,0,3,2,1:T(2,128)S(1)}, u32[]{:S(2)}, u32[]{:S(2)}) collective-permute-start(f32[2,1,16,1,2048]{4,0,3,2,1:T(2,128)S(1)} %get-tuple-element.77), channel_id=1, source_target_pairs={{0,1},{1,2},{2,3},{3,4},{4,5},{5,6},{6,7},{7,8},{8,9},{9,10},{10,1... | collective-permute-start | bytes 786440 | tf_op jit(solution)/shard_map/ppermute | solution.py:21
  65.0 25.8 %collective-permute-start.1 = (f32[2,1,16,1,2048]{4,0,3,2,1:T(2,128)S(1)}, f32[2,1,16,1,2048]{4,0,3,2,1:T(2,128)S(1)}, u32[]{:S(2)}, u32[]{:S(2)}) collective-permute-start(f32[2,1,16,1,2048]{4,0,3,2,1:T(2,128)S(1)} %get-tuple-element.91), channel_id=1, source_target_pairs={{1,0},{2,1},{3,2},{4,3},{5,4},{6,5},{7,6},{8,7},{9,8},{10,9},{11,1... | collective-permute-start | bytes 786440 | tf_op jit(solution)/shard_map/ppermute | solution.py:23
  119.7 11.4 %copy-start.11 = (f32[1,16,32,2048]{3,2,1,0:T(8,128)S(1)}, f32[1,16,32,2048]{3,2,1,0:T(8,128)}, u32[]{:S(2)}) copy-start(f32[1,16,32,2048]{3,2,1,0:T(8,128)} %param.19) | copy-start | bytes 12582916
  119.7 11.4 %copy-start.13 = (f32[1,16,32,2048]{3,0,2,1:T(1,128)S(1)}, f32[1,16,32,2048]{3,0,2,1:T(1,128)}, u32[]{:S(2)}) copy-start(f32[1,16,32,2048]{3,0,2,1:T(1,128)} %slice.452) | copy-start | bytes 12582916
  119.7 11.4 %copy-start.15 = (f32[1,16,32,2048]{3,0,2,1:T(1,128)S(1)}, f32[1,16,32,2048]{3,0,2,1:T(1,128)}, u32[]{:S(2)}) copy-start(f32[1,16,32,2048]{3,0,2,1:T(1,128)} %slice.456) | copy-start | bytes 12582916
  177.2 5.2 copy-start.18
  177.2 5.9 %copy-start.17 = (s32[32,2048]{1,0:T(8,128)S(1)}, s32[32,2048]{1,0:T(8,128)}, u32[]{:S(2)}) copy-start(s32[32,2048]{1,0:T(8,128)} %param.21) | copy-start | bytes 786436
  177.6 2.0 copy-start.3
  181.3 328.4 %all-gather.5.cloned.1.call-start = ((), (), s32[]{:S(2)}) async-start(), calls=%async_computation.1 | async-start | bytes 4718592 | tf_op jit(solution)/shard_map/all_gather | solution.py:90
  273.5 6.8 %copy-start.1 = (f32[16,32,2048]{2,1,0:T(8,128)S(1)}, f32[16,32,2048]{2,1,0:T(8,128)}, u32[]{:S(2)}) copy-start(f32[16,32,2048]{2,1,0:T(8,128)} %all-gather.3.cloned.1.call-done) | copy-start | bytes 12582916
  304.5 9.7 %copy-start.4 = (f32[1,16,32,2048]{3,0,2,1:T(1,128)S(1)}, f32[1,16,32,2048]{3,0,2,1:T(1,128)}, u32[]{:S(2)}) copy-start(f32[1,16,32,2048]{3,0,2,1:T(1,128)} %copy-done.3) | copy-start | bytes 12582916
  314.2 15.8 %copy-start.8 = (f32[1,1,16,32,2048]{4,0,3,2,1:T(1,128)S(1)}, f32[1,1,16,32,2048]{4,0,3,2,1:T(1,128)}, u32[]{:S(2)}) copy-start(f32[1,1,16,32,2048]{4,0,3,2,1:T(1,128)} %copy-done.7) | copy-start | bytes 12582916
  316.5 29.5 %copy-start.5 = (f32[1,16,32,2048]{3,0,2,1:T(1,128)}, f32[1,16,32,2048]{3,0,2,1:T(1,128)S(1)}, u32[]{:S(2)}) copy-start(f32[1,16,32,2048]{3,0,2,1:T(1,128)S(1)} %fusion.147) | copy-start | bytes 12582916
  316.9 7.2 %collective-permute-start.2 = (f32[2,1,16,1,2048]{4,0,3,2,1:T(2,128)S(1)}, f32[2,1,16,1,2048]{4,0,3,2,1:T(2,128)S(1)}, u32[]{:S(2)}, u32[]{:S(2)}) collective-permute-start(f32[2,1,16,1,2048]{4,0,3,2,1:T(2,128)S(1)} %get-tuple-element.89), channel_id=1, source_target_pairs={{0,1},{1,2},{2,3},{3,4},{4,5},{5,6},{6,7},{7,8},{8,9},{9,10},{10,1... | collective-permute-start | bytes 786440 | tf_op jit(solution)/shard_map/ppermute | solution.py:21
  320.9 9.2 %collective-permute-start.3 = (f32[2,1,16,1,2048]{4,0,3,2,1:T(2,128)S(1)}, f32[2,1,16,1,2048]{4,0,3,2,1:T(2,128)S(1)}, u32[]{:S(2)}, u32[]{:S(2)}) collective-permute-start(f32[2,1,16,1,2048]{4,0,3,2,1:T(2,128)S(1)} %get-tuple-element.90), channel_id=1, source_target_pairs={{1,0},{2,1},{3,2},{4,3},{5,4},{6,5},{7,6},{8,7},{9,8},{10,9},{11,1... | collective-permute-start | bytes 786440 | tf_op jit(solution)/shard_map/ppermute | solution.py:23
  359.2 11.4 %copy-start.6 = (f32[1,16,32,2048]{3,0,2,1:T(1,128)S(1)}, f32[1,16,32,2048]{3,0,2,1:T(1,128)}, u32[]{:S(2)}) copy-start(f32[1,16,32,2048]{3,0,2,1:T(1,128)} %copy-done.5) | copy-start | bytes 12582916
  359.2 11.4 %copy-start.12 = (f32[1,16,32,2048]{3,0,2,1:T(1,128)S(1)}, f32[1,16,32,2048]{3,0,2,1:T(1,128)}, u32[]{:S(2)}) copy-start(f32[1,16,32,2048]{3,0,2,1:T(1,128)} %slice.470) | copy-start | bytes 12582916
  359.2 11.4 %copy-start.14 = (f32[1,16,32,2048]{3,0,2,1:T(1,128)S(1)}, f32[1,16,32,2048]{3,0,2,1:T(1,128)}, u32[]{:S(2)}) copy-start(f32[1,16,32,2048]{3,0,2,1:T(1,128)} %slice.474) | copy-start | bytes 12582916
  413.8 2.0 copy-start.9
  509.7 6.8 %copy-start.2 = (f32[16,32,2048]{2,1,0:T(8,128)S(1)}, f32[16,32,2048]{2,1,0:T(8,128)}, u32[]{:S(2)}) copy-start(f32[16,32,2048]{2,1,0:T(8,128)} %all-gather.5.cloned.1.call-done) | copy-start | bytes 12582916
  540.6 9.7 %copy-start.10 = (f32[1,16,32,2048]{3,0,2,1:T(1,128)S(1)}, f32[1,16,32,2048]{3,0,2,1:T(1,128)}, u32[]{:S(2)}) copy-start(f32[1,16,32,2048]{3,0,2,1:T(1,128)} %copy-done.9) | copy-start | bytes 12582916
Sparse Core Ops, SparseCore 0:
  181.4 92.0 all-gather.2
  417.6 92.0 all-gather.4
where the time goes:
time: 567 us; the launch traced here: 563 us
  waiting for transfers between devices  189 us (33%)
  other arithmetic  180 us (32%)
  matrix products  105 us (19%)
  local copies, waits for them, and re-layouts  60.2 us (11%)
  starting transfers between devices  14.5 us (3%)
  between operations  14.2 us (3%)
    all_gather x2, waiting for transfers between devices, local(): gathered = lax.all_gather(planes, 'tier', axis=0, tiled=True)  182 us
    add x2, other arithmetic, local(): heating_snapshot = heating_snapshot + step_dt * conduct(padded_t, padded_k)  88.8 us
    dot_general x16, matrix products, select_solve(): jnp.einsum('ij,jxc->ixc', matrices[which], planes, precision=lax.Precisio...  81.2 us
    another operation x3, other arithmetic, local(): joined = padded(jnp.stack([heating_snapshot, kappa]), (('tile', 3),), 1)  45.7 us
    dot_general x1, matrix products, local(): jnp.dot(onehot.reshape(-1, POWER_TILES), dissipation_per_patch[0], precis...  23.6 us
    mul x2, other arithmetic, conduct(): 0.5 * (kcell[..., 1:, :, :] + kcell[..., :-1, :, :])  22.8 us
    concatenate x2, other arithmetic, padded(): jnp.concatenate([lax.ppermute(tail, axis, [(i, (i + 1) % count) for i in...  16.1 us
    slice x2, local copies, waits for them, and re-layouts, conduct(): centre = padded_t[..., 1:-1, :]  15.8 us
  transfers between devices with their start and end apart: 6, of which 4 were waited for; matrix products, arithmetic and copies ran while one was open for 5% of the time, Pallas kernels for 0%

commit v1 on v0

--- a/solution.py
+++ b/solution.py
@@ -8,6 +8,13 @@
 POWER_TILES = 128
 STEPS = 2
 step_dt = 0.04
+
+
+def gather_over(shard, axis, d):
+    count = lax.axis_size(axis)
+    parts = jnp.stack([shard for _ in range(count)])
+    parts = lax.all_to_all(parts, axis, split_axis=0, concat_axis=0)
+    return jnp.concatenate(parts, axis=d)
 
 
 def padded(cells, sides, width):
@@ -87,7 +94,7 @@
         heating_snapshot = heating_snapshot + step_dt * conduct(padded_t, padded_k)
         heating_snapshot = heating_snapshot.at[:, 0].add(step_dt * source)
         planes = jnp.stack([heating_snapshot[0, 0], heating_snapshot[0, -1]])
-        gathered = lax.all_gather(planes, "tier", axis=0, tiled=True)
+        gathered = gather_over(planes, "tier", 0)
         own_rows = lax.dynamic_slice_in_dim(glue_sheet_reciprocal_operators, 2 * tier_index, 2, 1)
         updated = select_solve(own_rows, gathered, glue_zone_label)
         heating_snapshot = heating_snapshot.at[0, 0].set(updated[0]).at[0, -1].set(updated[1])

time: 567 us -> 476 us (0.84)
  waiting for transfers between devices: 189 us -> 61.2 us
  blocking collectives: 0 us -> 51.9 us
  matrix products: 105 us -> 67.4 us
  local copies, waits for them, and re-layouts: 60.2 us -> 87.5 us
  between operations: 14.2 us -> 0.75 us
  starting transfers between devices: 14.5 us -> 20.7 us
    all_gather x2 -> x0, waiting for transfers between devices: 182 us -> none  [local(): gathered = lax.all_gather(planes, 'tier', axis=0, tiled=True)]
    all_to_all x0 -> x1, waiting for transfers between devices: none -> 53.9 us  [gather_over(): parts = lax.all_to_all(parts, axis, split_axis=0, concat_axis=0)]
    all_to_all x0 -> x1, blocking collectives: none -> 51.9 us  [gather_over(): parts = lax.all_to_all(parts, axis, split_axis=0, concat_axis=0)]
    dot_general x16, matrix products: 81.2 us -> 43.8 us  [select_solve(): jnp.einsum('ij,jxc->ixc', matrices[which], planes, precision=lax.Precisio...]
    reshape x0 -> x2, local copies, waits for them, and re-layouts: none -> 12.3 us  [gather_over(): return jnp.concatenate(parts, axis=d)]
    all_to_all x0 -> x2, local copies, waits for them, and re-layouts: none -> 10.9 us  [gather_over(): parts = lax.all_to_all(parts, axis, split_axis=0, concat_axis=0)]
    another operation x1 -> x3, local copies, waits for them, and re-layouts: 0.65 us -> 6.87 us  [the longest x2 6.3 us: gather_over(): parts = jnp.stack([shard for _ in range(count)])]
  transfers between devices with their start and end apart: 6 -> 5, of which waited for: 4 -> 3; matrix products, arithmetic and copies ran while one was open for 5% -> 5% of each run, Pallas kernels for 0% -> 0%
where the time goes in v1:
time: 476 us; the launch traced here: 470 us
  other arithmetic  180 us (38%)
  local copies, waits for them, and re-layouts  87.5 us (18%)
  matrix products  67.4 us (14%)
  waiting for transfers between devices  61.2 us (13%)
  blocking collectives  51.9 us (11%)
  starting transfers between devices  20.7 us (4%)
    add x2, other arithmetic, local(): heating_snapshot = heating_snapshot + step_dt * conduct(padded_t, padded_k)  88.8 us
    all_to_all x1, waiting for transfers between devices, gather_over(): parts = lax.all_to_all(parts, axis, split_axis=0, concat_axis=0)  53.9 us
    all_to_all x1, blocking collectives, gather_over(): parts = lax.all_to_all(parts, axis, split_axis=0, concat_axis=0)  51.9 us
    another operation x3, other arithmetic, local(): joined = padded(jnp.stack([heating_snapshot, kappa]), (('tile', 3),), 1)  45.6 us
    dot_general x16, matrix products, select_solve(): jnp.einsum('ij,jxc->ixc', matrices[which], planes, precision=lax.Precisio...  43.8 us
    dot_general x1, matrix products, local(): jnp.dot(onehot.reshape(-1, POWER_TILES), dissipation_per_patch[0], precis...  23.6 us
    mul x2, other arithmetic, conduct(): 0.5 * (kcell[..., 1:, :, :] + kcell[..., :-1, :, :])  22.8 us
    concatenate x2, other arithmetic, padded(): jnp.concatenate([lax.ppermute(tail, axis, [(i, (i + 1) % count) for i in...  16.5 us
  transfers between devices with their start and end apart: 5, of which 3 were waited for; matrix products, arithmetic and copies ran while one was open for 5% of the time, Pallas kernels for 0%

profile of v1, /device:TPU:27, one launch (start us, length us, event | category | flops | bytes accessed | tf_op | source)
XLA Modules:
  0.0 469.7 jit_solution(9638974551437191721)
XLA Ops:
  2.0 5.0 %stack.18 = f32[1,1,16,32,2048]{4,0,3,2,1:T(1,128)S(1)} reshape(f32[1,16,32,2048]{3,2,1,0:T(8,128)} %param.19) | data formatting | bytes 8388608 | tf_op jit(solution)/shard_map/stack | solution.py:91
  7.0 44.7 %fusion.8 = f32[1,1,16,32,2048]{4,0,3,2,1:T(1,128)S(1)} fusion(s32[1,16,32,2048]{3,2,1,0:T(8,128)S(1)} %copy-done.16, f32[]{:T(128)} %bitcast.15, f32[]{:T(128)} %bitcast.14, f32[]{:T(128)} %bitcast.13, f32[]{:T(128)} %bitcast.12, f32[]{:T(128)} %bitcast.11, f32[]{:T(128)} %bitcast.10, f32[]{:T(128)} %bitcast.9, f32[]{:T(128)} %bitcast.8, f32[]{:T(128)} %bitcast.7, ...), kind=kLoop, calls=%fused_computation.33 | loop fusion | flops 33554432 | bytes 8388672 | tf_op jit(solution)/shard_map/stack | solution.py:91
  52.3 6.1 %collective-permute-start = (f32[2,1,16,1,2048]{4,0,3,2,1:T(2,128)S(1)}, f32[2,1,16,1,2048]{4,0,3,2,1:T(2,128)S(1)}, u32[]{:S(2)}, u32[]{:S(2)}) collective-permute-start(f32[2,1,16,1,2048]{4,0,3,2,1:T(2,128)S(1)} %get-tuple-element.77), channel_id=1, source_target_pairs={{0,1},{1,2},{2,3},{3,4},{4,5},{5,6},{6,7},{7,8},{8,9},{9,10},{10,1... | collective-permute-start | bytes 786440 | tf_op jit(solution)/shard_map/ppermute | solution.py:28
  58.4 2.1 collective-permute-start.1
  60.5 23.6 %fusion.1 = f32[1,32,2048]{2,0,1:T(1,128)S(1)} fusion(s32[32,2048]{1,0:T(8,128)S(1)} %bitcast.130, f32[1,128]{1,0:T(1,128)S(1)} %copy-done.20), kind=kOutput, calls=%fused_computation.2 | convolution fusion | flops 109051904 | bytes 524800 | tf_op jit(solution)/shard_map/dot_general | solution.py:84
  84.2 8.0 %fusion.5 = f32[2,1,16,34,2048]{4,0,3,2,1:T(2,128)S(1)} fusion(f32[1,1,16,32,2048]{4,0,3,2,1:T(1,128)S(1)} %fusion.8, f32[2,1,16,1,2048]{4,0,3,2,1:T(2,128)S(1)} %collective-permute-done.1, f32[1,1,16,32,2048]{4,0,3,2,1:T(1,128)S(1)} %stack.18, f32[2,1,16,1,2048]{4,0,3,2,1:T(2,128)S(1)} %collective-permute-done), kind=kLoop, calls=%fused_computation.23 | loop fusion | flops 6684672 | bytes 17825792 | tf_op jit(solution)/shard_map/concatenate | solution.py:26
  92.2 7.9 %slice_bitcast_fusion.3 = (f32[1,16,34,2048]{3,0,2,1:T(1,128)S(1)}, f32[1,16,34,2048]{3,0,2,1:T(1,128)}) fusion(f32[2,1,16,34,2048]{4,0,3,2,1:T(2,128)S(1)} %fusion.5), kind=kLoop, calls=%fused_computation.32 | loop fusion | bytes 17825792 | tf_op jit(solution)/shard_map/squeeze | solution.py:93
  100.1 5.2 %slice.452 = f32[1,16,32,2048]{3,0,2,1:T(1,128)} slice(f32[1,16,34,2048]{3,0,2,1:T(1,128)S(1)} %get-tuple-element.83), slice={[0:1], [0:16], [1:33], [0:2048]} | slice | bytes 8388608 | tf_op jit(solution)/shard_map/slice | solution.py:45
  105.3 7.9 %slice.456 = f32[1,16,32,2048]{3,0,2,1:T(1,128)} slice(f32[1,16,34,2048]{3,0,2,1:T(1,128)} %get-tuple-element.84), slice={[0:1], [0:16], [1:33], [0:2048]} | slice | bytes 8388608 | tf_op jit(solution)/shard_map/slice | solution.py:44
  113.2 11.4 %fusion.21 = f32[1,15,32,2048]{3,0,2,1:T(1,128)S(1)} fusion(f32[1,16,34,2048]{3,0,2,1:T(1,128)} %get-tuple-element.84, f32[1,16,34,2048]{3,0,2,1:T(1,128)S(1)} %get-tuple-element.83), kind=kLoop, calls=%fused_computation.59 | loop fusion | flops 3932160 | bytes 19660800 | tf_op jit(solution)/shard_map/mul | solution.py:53
  124.6 46.4 %copy_add_fusion = f32[1,16,32,2048]{3,0,2,1:T(1,128)S(1)} fusion(f32[1,16,32,2048]{3,2,1,0:T(8,128)S(1)} %copy-done.11, f32[1,15,32,2048]{3,0,2,1:T(1,128)S(1)} %fusion.21, f32[1,16,32,2048]{3,0,2,1:T(1,128)S(1)} %copy-done.15, f32[1,16,32,2048]{3,0,2,1:T(1,128)S(1)} %copy-done.13, f32[1,16,34,2048]{3,0,2,1:T(1,128)} %get-tuple-element.84, ...), kind=kLoop, calls=%fused_computation.52 | loop fusion | flops 24117248 | bytes 37486592 | tf_op jit(solution)/shard_map/add | solution.py:94
  171.4 2.0 copy-done.3
  173.9 4.2 stack.22
  178.1 4.7 %all-to-all-start = ((f32[8,2,32,2048]{3,1,2,0:T(2,128)}), f32[8,2,32,2048]{3,1,2,0:T(2,128)}, u32[]{:S(2)}, u32[]{:S(2)}) async-start(f32[8,2,32,2048]{3,1,2,0:T(2,128)} %stack.22), calls=%async_computation | async-start | bytes 8388608 | tf_op jit(solution)/shard_map/all_to_all | solution.py:16
  184.5 53.9 %all-to-all-done = f32[8,2,32,2048]{3,1,2,0:T(2,128)} async-done(((f32[8,2,32,2048]{3,1,2,0:T(2,128)}), f32[8,2,32,2048]{3,1,2,0:T(2,128)}, u32[]{:S(2)}, u32[]{:S(2)}) %all-to-all-start) | async-done | bytes 4194336 | tf_op jit(solution)/shard_map/all_to_all | solution.py:16
  238.5 7.0 %copy.61 = f32[8,2,32,2048]{3,1,0,2:T(2,128)} copy(f32[8,2,32,2048]{3,1,2,0:T(2,128)} %all-to-all-done) | data formatting | bytes 8388608 | tf_op jit(solution)/shard_map/all_to_all | solution.py:16
  245.5 6.0 %reshape.256 = f32[16,32,2048]{2,0,1:T(8,128)} reshape(f32[8,2,32,2048]{3,1,0,2:T(2,128)} %copy.61) | data formatting | bytes 8388608 | tf_op jit(solution)/shard_map/reshape | solution.py:17
  251.5 4.6 convolution_select_fusion.13
  256.2 2.3 convolution_select_fusion.14
  258.5 2.3 convolution_select_fusion.11
  260.8 2.3 convolution_select_fusion.9
  263.1 2.8 fusion.24
  265.8 2.6 fusion.26
  268.4 2.6 fusion.28
  271.0 2.5 fusion.29
  273.7 2.0 fusion.39
  276.1 5.9 %collective-permute-start.2 = (f32[2,1,16,1,2048]{4,0,3,2,1:T(2,128)S(1)}, f32[2,1,16,1,2048]{4,0,3,2,1:T(2,128)S(1)}, u32[]{:S(2)}, u32[]{:S(2)}) collective-permute-start(f32[2,1,16,1,2048]{4,0,3,2,1:T(2,128)S(1)} %get-tuple-element.89), channel_id=1, source_target_pairs={{0,1},{1,2},{2,3},{3,4},{4,5},{5,6},{6,7},{7,8},{8,9},{9,10},{10,1... | collective-permute-start | bytes 786440 | tf_op jit(solution)/shard_map/ppermute | solution.py:28
  285.3 5.9 %collective-permute-done.3 = f32[2,1,16,1,2048]{4,0,3,2,1:T(2,128)S(1)} collective-permute-done((f32[2,1,16,1,2048]{4,0,3,2,1:T(2,128)S(1)}, f32[2,1,16,1,2048]{4,0,3,2,1:T(2,128)S(1)}, u32[]{:S(2)}, u32[]{:S(2)}) %collective-permute-start.3) | collective-permute-done | bytes 262176 | tf_op jit(solution)/shard_map/ppermute | solution.py:30
  291.2 8.5 %fusion.7 = f32[2,1,16,34,2048]{4,0,3,2,1:T(2,128)S(1)} fusion(f32[1,1,16,32,2048]{4,0,3,2,1:T(1,128)S(1)} %copy-done.8, f32[2,1,16,1,2048]{4,0,3,2,1:T(2,128)S(1)} %collective-permute-done.3, f32[1,1,16,32,2048]{4,0,3,2,1:T(1,128)S(1)} %bitcast.129, f32[2,1,16,1,2048]{4,0,3,2,1:T(2,128)S(1)} %collective-permute-done.2), kind=kLoop, calls=%fused_computation.25 | loop fusion | flops 6684672 | bytes 17825792 | tf_op jit(solution)/shard_map/concatenate | solution.py:26
  299.7 7.9 %slice_bitcast_fusion.1 = (f32[1,16,34,2048]{3,0,2,1:T(1,128)S(1)}, f32[1,16,34,2048]{3,0,2,1:T(1,128)}) fusion(f32[2,1,16,34,2048]{4,0,3,2,1:T(2,128)S(1)} %fusion.7), kind=kLoop, calls=%fused_computation.30 | loop fusion | bytes 17825792 | tf_op jit(solution)/shard_map/squeeze | solution.py:93
  307.6 5.2 %slice.470 = f32[1,16,32,2048]{3,0,2,1:T(1,128)} slice(f32[1,16,34,2048]{3,0,2,1:T(1,128)S(1)} %get-tuple-element.81), slice={[0:1], [0:16], [1:33], [0:2048]} | slice | bytes 8388608 | tf_op jit(solution)/shard_map/slice | solution.py:45
  312.8 7.9 %slice.474 = f32[1,16,32,2048]{3,0,2,1:T(1,128)} slice(f32[1,16,34,2048]{3,0,2,1:T(1,128)} %get-tuple-element.82), slice={[0:1], [0:16], [1:33], [0:2048]} | slice | bytes 8388608 | tf_op jit(solution)/shard_map/slice | solution.py:44
  320.7 11.4 %fusion.19 = f32[1,15,32,2048]{3,0,2,1:T(1,128)S(1)} fusion(f32[1,16,34,2048]{3,0,2,1:T(1,128)} %get-tuple-element.82, f32[1,16,34,2048]{3,0,2,1:T(1,128)S(1)} %get-tuple-element.81), kind=kLoop, calls=%fused_computation.55 | loop fusion | flops 3932160 | bytes 19660800 | tf_op jit(solution)/shard_map/mul | solution.py:53
  332.1 42.4 %multiply_add_fusion = f32[1,16,32,2048]{3,0,2,1:T(1,128)S(1)} fusion(f32[1,16,32,2048]{3,0,2,1:T(1,128)S(1)} %copy-done.6, f32[1,15,32,2048]{3,0,2,1:T(1,128)S(1)} %fusion.19, f32[1,16,32,2048]{3,0,2,1:T(1,128)S(1)} %copy-done.14, f32[1,16,32,2048]{3,0,2,1:T(1,128)S(1)} %copy-done.12, f32[1,16,34,2048]{3,0,2,1:T(1,128)} %get-tuple-element.82, ...), kind=kLoop, calls=%fused_computation.53 | loop fusion | flops 24117248 | bytes 37486592 | tf_op jit(solution)/shard_map/add | solution.py:94
  375.0 2.0 copy-done.9
  377.5 2.1 stack.52
  379.6 51.9 %all_to_all.10 = f32[8,2,32,2048]{3,1,2,0:T(2,128)S(1)} all-to-all(f32[8,2,32,2048]{3,1,2,0:T(2,128)S(1)} %stack.52), channel_id=1, replica_groups=mesh['tier'=8,'tile'=16] {'tier'}, dimensions={0} | all-to-all | bytes 8388608 | tf_op jit(solution)/shard_map/all_to_all | solution.py:16
  431.6 3.9 copy.62
  435.4 6.3 %reshape.260 = f32[16,32,2048]{2,0,1:T(8,128)} reshape(f32[8,2,32,2048]{3,1,0,2:T(2,128)} %copy.62) | data formatting | bytes 8388608 | tf_op jit(solution)/shard_map/reshape | solution.py:17
  441.7 4.6 convolution_select_fusion.5
  446.4 2.3 convolution_select_fusion.6
  448.7 2.3 convolution_select_fusion.3
  450.9 2.3 convolution_select_fusion.1
  453.2 2.8 fusion.31
  456.1 2.6 fusion.33
  458.7 2.6 fusion.35
  461.3 2.5 fusion.36
  465.6 4.0 copy.63
  (61 shorter events, 11.8 us)
Async XLA Ops:
  0.0 251.5 %copy-start = (f32[8,16,16]{2,1,0:T(8,128)S(1)}, f32[8,16,16]{2,1,0:T(8,128)}, u32[]{:S(2)}) copy-start(f32[8,16,16]{2,1,0:T(8,128)} %param.25) | copy-start | bytes 24580
  1.9 5.0 %copy-start.16 = (s32[1,16,32,2048]{3,2,1,0:T(8,128)S(1)}, s32[1,16,32,2048]{3,2,1,0:T(8,128)}, u32[]{:S(2)}) copy-start(s32[1,16,32,2048]{3,2,1,0:T(8,128)} %param.20) | copy-start | bytes 12582916
  51.7 32.5 %copy-start.7 = (f32[1,1,16,32,2048]{4,0,3,2,1:T(1,128)}, f32[1,1,16,32,2048]{4,0,3,2,1:T(1,128)S(1)}, u32[]{:S(2)}) copy-start(f32[1,1,16,32,2048]{4,0,3,2,1:T(1,128)S(1)} %fusion.8) | copy-start | bytes 12582916
  51.7 8.8 %copy-start.19 = (s32[1,32,2048]{2,1,0:T(8,128)S(1)}, s32[1,32,2048]{2,1,0:T(8,128)}, u32[]{:S(2)}) copy-start(s32[1,32,2048]{2,1,0:T(8,128)} %param.22) | copy-start | bytes 786436
  51.7 8.8 %copy-start.20 = (f32[1,128]{1,0:T(1,128)S(1)}, f32[1,128]{1,0:T(1,128)}, u32[]{:S(2)}) copy-start(f32[1,128]{1,0:T(1,128)} %param.24) | copy-start | bytes 1540
  52.3 31.9 %collective-permute-start = (f32[2,1,16,1,2048]{4,0,3,2,1:T(2,128)S(1)}, f32[2,1,16,1,2048]{4,0,3,2,1:T(2,128)S(1)}, u32[]{:S(2)}, u32[]{:S(2)}) collective-permute-start(f32[2,1,16,1,2048]{4,0,3,2,1:T(2,128)S(1)} %get-tuple-element.77), channel_id=1, source_target_pairs={{0,1},{1,2},{2,3},{3,4},{4,5},{5,6},{6,7},{7,8},{8,9},{9,10},{10,1... | collective-permute-start | bytes 786440 | tf_op jit(solution)/shard_map/ppermute | solution.py:28
  58.4 25.8 %collective-permute-start.1 = (f32[2,1,16,1,2048]{4,0,3,2,1:T(2,128)S(1)}, f32[2,1,16,1,2048]{4,0,3,2,1:T(2,128)S(1)}, u32[]{:S(2)}, u32[]{:S(2)}) collective-permute-start(f32[2,1,16,1,2048]{4,0,3,2,1:T(2,128)S(1)} %get-tuple-element.91), channel_id=1, source_target_pairs={{1,0},{2,1},{3,2},{4,3},{5,4},{6,5},{7,6},{8,7},{9,8},{10,9},{11,1... | collective-permute-start | bytes 786440 | tf_op jit(solution)/shard_map/ppermute | solution.py:30
  113.1 11.4 %copy-start.11 = (f32[1,16,32,2048]{3,2,1,0:T(8,128)S(1)}, f32[1,16,32,2048]{3,2,1,0:T(8,128)}, u32[]{:S(2)}) copy-start(f32[1,16,32,2048]{3,2,1,0:T(8,128)} %param.19) | copy-start | bytes 12582916
  113.1 11.4 %copy-start.13 = (f32[1,16,32,2048]{3,0,2,1:T(1,128)S(1)}, f32[1,16,32,2048]{3,0,2,1:T(1,128)}, u32[]{:S(2)}) copy-start(f32[1,16,32,2048]{3,0,2,1:T(1,128)} %slice.452) | copy-start | bytes 12582916
  113.2 11.4 %copy-start.15 = (f32[1,16,32,2048]{3,0,2,1:T(1,128)S(1)}, f32[1,16,32,2048]{3,0,2,1:T(1,128)}, u32[]{:S(2)}) copy-start(f32[1,16,32,2048]{3,0,2,1:T(1,128)} %slice.456) | copy-start | bytes 12582916
  171.4 2.0 copy-start.3
  178.1 5.3 %copy-start.18 = (s32[4]{0:T(128)S(1)}, s32[4]{0:T(128)}, u32[]{:S(2)}) copy-start(s32[4]{0:T(128)} %constant.201.clone.1) | copy-start | bytes 52
  178.1 6.1 %copy-start.17 = (s32[32,2048]{1,0:T(8,128)S(1)}, s32[32,2048]{1,0:T(8,128)}, u32[]{:S(2)}) copy-start(s32[32,2048]{1,0:T(8,128)} %param.21) | copy-start | bytes 786436
  178.1 60.4 %all-to-all-start = ((f32[8,2,32,2048]{3,1,2,0:T(2,128)}), f32[8,2,32,2048]{3,1,2,0:T(2,128)}, u32[]{:S(2)}, u32[]{:S(2)}) async-start(f32[8,2,32,2048]{3,1,2,0:T(2,128)} %stack.22), calls=%async_computation | async-start | bytes 8388608 | tf_op jit(solution)/shard_map/all_to_all | solution.py:16
  251.5 4.6 copy-start.2
  268.4 5.1 %copy-start.4 = (f32[1,16,32,2048]{3,0,2,1:T(1,128)S(1)}, f32[1,16,32,2048]{3,0,2,1:T(1,128)}, u32[]{:S(2)}) copy-start(f32[1,16,32,2048]{3,0,2,1:T(1,128)} %copy-done.3) | copy-start | bytes 12582916
  273.5 17.7 %copy-start.8 = (f32[1,1,16,32,2048]{4,0,3,2,1:T(1,128)S(1)}, f32[1,1,16,32,2048]{4,0,3,2,1:T(1,128)}, u32[]{:S(2)}) copy-start(f32[1,1,16,32,2048]{4,0,3,2,1:T(1,128)} %copy-done.7) | copy-start | bytes 12582916
  275.7 31.9 %copy-start.5 = (f32[1,16,32,2048]{3,0,2,1:T(1,128)}, f32[1,16,32,2048]{3,0,2,1:T(1,128)S(1)}, u32[]{:S(2)}) copy-start(f32[1,16,32,2048]{3,0,2,1:T(1,128)S(1)} %fusion.39) | copy-start | bytes 12582916
  276.1 9.2 %collective-permute-start.2 = (f32[2,1,16,1,2048]{4,0,3,2,1:T(2,128)S(1)}, f32[2,1,16,1,2048]{4,0,3,2,1:T(2,128)S(1)}, u32[]{:S(2)}, u32[]{:S(2)}) collective-permute-start(f32[2,1,16,1,2048]{4,0,3,2,1:T(2,128)S(1)} %get-tuple-element.89), channel_id=1, source_target_pairs={{0,1},{1,2},{2,3},{3,4},{4,5},{5,6},{6,7},{7,8},{8,9},{9,10},{10,1... | collective-permute-start | bytes 786440 | tf_op jit(solution)/shard_map/ppermute | solution.py:28
  282.0 9.2 %collective-permute-start.3 = (f32[2,1,16,1,2048]{4,0,3,2,1:T(2,128)S(1)}, f32[2,1,16,1,2048]{4,0,3,2,1:T(2,128)S(1)}, u32[]{:S(2)}, u32[]{:S(2)}) collective-permute-start(f32[2,1,16,1,2048]{4,0,3,2,1:T(2,128)S(1)} %get-tuple-element.90), channel_id=1, source_target_pairs={{1,0},{2,1},{3,2},{4,3},{5,4},{6,5},{7,6},{8,7},{9,8},{10,9},{11,1... | collective-permute-start | bytes 786440 | tf_op jit(solution)/shard_map/ppermute | solution.py:30
  320.7 11.4 %copy-start.6 = (f32[1,16,32,2048]{3,0,2,1:T(1,128)S(1)}, f32[1,16,32,2048]{3,0,2,1:T(1,128)}, u32[]{:S(2)}) copy-start(f32[1,16,32,2048]{3,0,2,1:T(1,128)} %copy-done.5) | copy-start | bytes 12582916
  320.7 11.4 %copy-start.12 = (f32[1,16,32,2048]{3,0,2,1:T(1,128)S(1)}, f32[1,16,32,2048]{3,0,2,1:T(1,128)}, u32[]{:S(2)}) copy-start(f32[1,16,32,2048]{3,0,2,1:T(1,128)} %slice.470) | copy-start | bytes 12582916
  320.7 11.4 %copy-start.14 = (f32[1,16,32,2048]{3,0,2,1:T(1,128)S(1)}, f32[1,16,32,2048]{3,0,2,1:T(1,128)}, u32[]{:S(2)}) copy-start(f32[1,16,32,2048]{3,0,2,1:T(1,128)} %slice.474) | copy-start | bytes 12582916
  375.0 2.0 copy-start.9
  441.7 4.6 copy-start.1
  458.6 5.1 %copy-start.10 = (f32[1,16,32,2048]{3,0,2,1:T(1,128)S(1)}, f32[1,16,32,2048]{3,0,2,1:T(1,128)}, u32[]{:S(2)}) copy-start(f32[1,16,32,2048]{3,0,2,1:T(1,128)} %copy-done.9) | copy-start | bytes 12582916
